TPU v7x, 32 devices: a whole 2x2x4 slice. The times are simulated.
32 devices in a mesh: groups: 2 (over y), seq: 8 (over z, x), tensor: 2 (over core).
Axes of the slice: x: 2, y: 2, z: 4, core: 2. Of those that a mesh axis runs over, the one named last changes fastest.
Arguments:
- queries: bfloat16 [2048, 1536], P(('groups', 'seq'), 'tensor'), parts along dimension 0, may hold values from -64 to 64
- keys: bfloat16 [2048, 1536], P(('groups', 'seq'), 'tensor'), parts along dimension 0, may hold values from -6 to 6
- values: bfloat16 [2048, 1536], P(('groups', 'seq'), 'tensor'), parts along dimension 0, may hold values from -6 to 6
- text_keys: bfloat16 [64, 1536], P(('groups', 'seq'), 'tensor'), parts along dimension 0, may hold values from -6 to 6
- text_values: bfloat16 [64, 1536], P(('groups', 'seq'), 'tensor'), parts along dimension 0, may hold values from -6 to 6
- conv_weight: bfloat16 [4, 1536], P(None, 'tensor'), may hold values from -3 to 3
- out_weight: bfloat16 [1536, 1536], P('tensor'), may hold values from -0.15625 to 0.15625
- image_hidden: bfloat16 [2048, 1536], P(('groups', 'seq')), parts along dimension 0, may hold values from -6 to 6
- gate: bfloat16 [3072], P('groups'), parts along dimension 0, may hold values from -8 to 8
Outputs:
- mixed: bfloat16 [2048, 1536], P(('groups', 'seq')), parts along dimension 0
There are 2 independent parts, one for each index of `groups`. A program takes and returns all parts, laid end to end along the dimension named above; an argument that names none is the same for every part. Nothing has to cross between parts.
All inputs are finite; a program needn't handle non-finite values.
Results may differ from a plain program's by a relative error of at most 0.011.
Values may be sent and summed in bfloat16 or wider, within the bound.
A program may use at most 64 MiB of HBM per device.

v0:
```python
import math
import jax
import jax.numpy as jnp
from jax import lax
from jax.sharding import PartitionSpec as P

HEAD_DIM = 128
key_block = 512


def rope_angles(row_pos, col_pos, head_dim):
    lead_dims = head_dim // 8
    group_dims = head_dim * 7 // 16
    frequency = 10000.0 ** (-(2.0 * jnp.arange(group_dims // 2, dtype=jnp.float32)) / group_dims)
    zero_angles = jnp.zeros((row_pos.shape[0], lead_dims // 2), jnp.float32)
    return jnp.concatenate(
        [zero_angles, row_pos[:, None] * frequency[None, :], col_pos[:, None] * frequency[None, :]],
        axis=1,
    )


def apply_rope(field, angles):
    paired = field.reshape(field.shape[0], field.shape[1], field.shape[2] // 2, 2)
    even_part = paired[..., 0]
    odd_part = paired[..., 1]
    cos_part = jnp.cos(angles)[:, None, :]
    sin_part = jnp.sin(angles)[:, None, :]
    turned = jnp.stack(
        [even_part * cos_part - odd_part * sin_part, even_part * sin_part + odd_part * cos_part],
        axis=-1,
    )
    return turned.reshape(field.shape)


def compress(field, taps, row_width):
    features = field.shape[1]
    grid_cells = field.astype(jnp.float32).reshape(2, row_width // 2, 2, features)
    tap_grid = taps.astype(jnp.float32).reshape(2, 2, features)
    return (
        grid_cells[0, :, 0] * tap_grid[0, 0]
        + grid_cells[0, :, 1] * tap_grid[0, 1]
        + grid_cells[1, :, 0] * tap_grid[1, 0]
        + grid_cells[1, :, 1] * tap_grid[1, 1]
    )


def absorb_block(carry, key_rows, value_rows, queries_rot):
    row_max, row_total, accumulated = carry
    heads_dev = queries_rot.shape[1]
    key_heads = key_rows.reshape(key_rows.shape[0], heads_dev, -1)
    value_heads = value_rows.reshape(value_rows.shape[0], heads_dev, -1)
    scores = jnp.einsum(
        "qhd,khd->hqk", queries_rot, key_heads, preferred_element_type=jnp.float32
    ) * (1.0 / math.sqrt(HEAD_DIM))
    new_max = jnp.maximum(row_max, jnp.max(scores, axis=-1))
    rescale = jnp.exp(row_max - new_max)
    weights = jnp.exp(scores - new_max[:, :, None]).astype(jnp.bfloat16)
    row_total = row_total * rescale + jnp.sum(weights.astype(jnp.float32), axis=-1)
    mixed_values = jnp.einsum(
        "hqk,khd->qhd", weights, value_heads, preferred_element_type=jnp.float32
    )
    accumulated = accumulated * rescale.T[:, :, None] + mixed_values
    return (new_max, row_total, accumulated)


def absorb(carry, key_rows, value_rows, queries_rot):
    key_count = key_rows.shape[0]
    if key_count > key_block and key_count % key_block == 0:
        stacked_keys = key_rows.reshape(key_count // key_block, key_block, key_rows.shape[1])
        stacked_values = value_rows.reshape(key_count // key_block, key_block, value_rows.shape[1])

        def one_step(running, block_pair):
            return (absorb_block(running, block_pair[0], block_pair[1], queries_rot), None)

        carry, unused = lax.scan(one_step, carry, (stacked_keys, stacked_values))
        return carry
    return absorb_block(carry, key_rows, value_rows, queries_rot)


def local(
    queries, keys, values, text_keys, text_values, conv_weight, out_weight, image_hidden, gate
):
    local_tokens, features = queries.shape
    row_width = local_tokens // 2
    heads_dev = features // HEAD_DIM
    seq_place = lax.axis_index("seq").astype(jnp.float32)
    token_ids = jnp.arange(local_tokens, dtype=jnp.int32)
    query_rows = 2.0 * seq_place + (token_ids // row_width).astype(jnp.float32)
    query_cols = (token_ids % row_width).astype(jnp.float32)
    queries_rot = apply_rope(
        queries.astype(jnp.float32).reshape(local_tokens, heads_dev, HEAD_DIM),
        rope_angles(query_rows, query_cols, HEAD_DIM),
    ).astype(jnp.bfloat16)
    patch_ids = jnp.arange(row_width // 2, dtype=jnp.int32).astype(jnp.float32)
    patch_rows = 2.0 * seq_place + 0.5 + 0.0 * patch_ids
    patch_cols = 2.0 * patch_ids + 0.5
    short_keys = (
        apply_rope(
            compress(keys, conv_weight, row_width).reshape(row_width // 2, heads_dev, HEAD_DIM),
            rope_angles(patch_rows, patch_cols, HEAD_DIM),
        )
        .astype(jnp.bfloat16)
        .reshape(row_width // 2, features)
    )
    short_values = compress(values, conv_weight, row_width).astype(jnp.bfloat16)
    initial = (
        jnp.full((heads_dev, local_tokens), -1e30, jnp.float32),
        jnp.zeros((heads_dev, local_tokens), jnp.float32),
        jnp.zeros((local_tokens, heads_dev, HEAD_DIM), jnp.float32),
    )
    all_text_keys, all_text_values = (
        lax.all_gather(text_keys, "seq", axis=0, tiled=True),
        lax.all_gather(text_values, "seq", axis=0, tiled=True),
    )
    after_text = absorb(initial, all_text_keys, all_text_values, queries_rot)
    row_max, row_total, accumulated = absorb(
        after_text,
        lax.all_gather(short_keys, "seq", axis=0, tiled=True),
        lax.all_gather(short_values, "seq", axis=0, tiled=True),
        queries_rot,
    )
    attended = (
        (accumulated / row_total.T[:, :, None]).astype(jnp.bfloat16).reshape(local_tokens, features)
    )
    projected = lax.psum(
        jnp.dot(attended, out_weight, preferred_element_type=jnp.float32).astype(jnp.bfloat16),
        "tensor",
    ).astype(jnp.float32)
    return (
        image_hidden.astype(jnp.float32) + gate.astype(jnp.float32)[None, :] * projected
    ).astype(jnp.bfloat16)


def solution(mesh):
    placed = (
        P(("groups", "seq"), "tensor"),
        P(("groups", "seq"), "tensor"),
        P(("groups", "seq"), "tensor"),
        P(("groups", "seq"), "tensor"),
        P(("groups", "seq"), "tensor"),
        P(None, "tensor"),
        P("tensor", None),
        P(("groups", "seq"), None),
        P("groups"),
    )
    return jax.shard_map(
        local, mesh=mesh, in_specs=placed, out_specs=P(("groups", "seq"), None), check_vma=False
    )
```

profile of v0, /device:TPU:0, one launch (start us, length us, event | category | flops | bytes accessed | tf_op | source)
XLA Modules:
  0.0 191.8 jit_solution(10425235532652120512)
XLA Ops:
  7.1 0.6 fusion.22
  7.6 0.7 reshape.261
  8.4 0.8 mul.304
  9.2 0.8 mul.307
  10.1 0.8 mul.310
  10.9 0.8 mul.313
  11.7 1.1 reshape.259
  12.9 1.0 fusion.27
  14.2 1.1 copy.64
  15.2 1.8 copy.65
  17.0 0.6 fusion.24
  17.6 0.7 broadcast_multiply_fusion.1
  18.5 3.4 %multiply_add_fusion = f32[32,6,64,2]{0,3,2,1:T(2,128)S(1)} fusion(f32[32,6,64,2]{0,3,2,1:T(2,128)S(1)} %bitcast.86, f32[32,6,64,2]{0,3,2,1:T(2,128)} %bitcast.89, f32[32,6,64,2]{0,3,2,1:T(2,128)S(1)} %bitcast.88, f32[32,6,64,2]{0,3,2,1:T(2,128)S(1)} %bitcast.87, f32[6,64,2]{2,1,0:T(8,128)} %mul.313, f32[6,64,2]{2,1,0:T(8,128)} %mul.310, ...), kind=kLoop, calls=%fused_computation.13 | loop fusion | flops 172032 | bytes 503808 | tf_op jit(solution)/shard_map/add | solution.py:40
  22.5 0.5 pad_maximum_fusion.1
  23.1 32.8 %all_gather.14 = bf16[256,768]{1,0:T(8,128)(2,1)S(1)} all-gather(bf16[32,768]{1,0:T(8,128)(2,1)S(1)} %copy.51), channel_id=1, replica_groups=mesh['groups'=2,'seq'=8,'tensor'=2] {'seq'}, dimensions={0}, use_global_device_ids=true | all-gather | bytes 442368 | tf_op jit(solution)/shard_map/all_gather | solution.py:118
  56.4 31.0 %all-gather = bf16[8,4,768]{2,1,0:T(4,128)(2,1)S(1)} all-gather(bf16[1,4,768]{2,1,0:T(4,128)(2,1)} %bitcast.93), channel_id=1, replica_groups=mesh['groups'=2,'seq'=8,'tensor'=2] {'seq'}, dimensions={0}, use_global_device_ids=true | all-gather | bytes 55296 | tf_op jit(solution)/shard_map/all_gather | solution.py:112
  87.4 0.7 reshape.246
  88.0 0.8 broadcast_multiply_fusion.3
  88.8 0.8 fusion.17
  90.6 1.0 fusion.30
  91.5 1.4 fusion.29
  92.9 1.1 reshape.263
  94.4 31.0 %all_gather.15 = bf16[256,768]{1,0:T(8,128)(2,1)S(1)} all-gather(bf16[32,768]{1,0:T(8,128)(2,1)S(1)} %fusion.8), channel_id=1, replica_groups=mesh['groups'=2,'seq'=8,'tensor'=2] {'seq'}, dimensions={0}, use_global_device_ids=true | all-gather | bytes 442368 | tf_op jit(solution)/shard_map/all_gather | solution.py:119
  125.4 0.9 copy.58
  126.3 0.7 broadcast_maximum_fusion
  127.3 2.1 %convolution_bitcast_fusion.1 = f32[128,6,128]{0,2,1:T(8,128)} fusion(bf16[256,6,128]{0,2,1:T(8,128)(2,1)} %bitcast.85, f32[6,128,256]{2,1,0:T(8,128)S(1)} %get-tuple-element.37, f32[6,128]{1,0:T(8,128)S(1)} %get-tuple-element.29), kind=kOutput, calls=%fused_computation.4 | convolution fusion | flops 50724864 | bytes 1575936 | tf_op jit(solution)/shard_map/hqk,khd->qhd/dot_general | solution.py:59
  129.4 30.8 %all-gather.1 = bf16[8,4,768]{2,1,0:T(4,128)(2,1)S(1)} all-gather(bf16[1,4,768]{2,1,0:T(4,128)(2,1)S(1)} %bitcast.94), channel_id=1, replica_groups=mesh['groups'=2,'seq'=8,'tensor'=2] {'seq'}, dimensions={0}, use_global_device_ids=true | all-gather | bytes 55296 | tf_op jit(solution)/shard_map/all_gather | solution.py:113
  160.3 0.7 bitcast_add_fusion
  161.0 1.4 fusion.4
  162.4 1.2 convolution_convert_fusion
  163.7 19.4 %all-reduce.2.cloned.1.call-done = bf16[128,1536]{1,0:T(8,128)(2,1)} async-done(((bf16[128,1536]{1,0:T(8,128)(2,1)}), bf16[128,1536]{1,0:T(8,128)(2,1)}) %all-reduce.2.cloned.1.call-update) | async-done | bytes 393232 | tf_op jit(solution)/shard_map/psum | solution.py:125
  183.1 1.9 add_convert_fusion
  (39 shorter events, 4.0 us)
Async XLA Ops:
  6.5 155.8 %copy-start = (bf16[768,1536]{1,0:T(8,128)(2,1)S(1)}, bf16[768,1536]{1,0:T(8,128)(2,1)}, u32[]{:S(2)}) copy-start(bf16[768,1536]{1,0:T(8,128)(2,1)} %param.15) | copy-start | bytes 7077892
  6.5 176.6 %all-reduce.2.cloned.1.call-start = ((), (), s32[]{:S(2)}) async-start(), calls=%async_computation | async-start | bytes 786432 | tf_op jit(solution)/shard_map/psum | solution.py:125
  17.6 0.9 copy-start.7
  21.9 34.1 %copy-start.4 = (bf16[128,768]{1,0:T(8,128)(2,1)S(1)}, bf16[128,768]{1,0:T(8,128)(2,1)}, u32[]{:S(2)}) copy-start(bf16[128,768]{1,0:T(8,128)(2,1)} %param.9) | copy-start | bytes 589828
  88.0 3.5 %copy-start.3 = (bf16[32,6,128]{2,1,0:T(8,128)(2,1)S(1)}, bf16[32,6,128]{2,1,0:T(8,128)(2,1)}, u32[]{:S(2)}) copy-start(bf16[32,6,128]{2,1,0:T(8,128)(2,1)} %reshape.246) | copy-start | bytes 147460
  94.4 35.0 %copy-start.5 = (bf16[4,768]{1,0:T(4,128)(2,1)S(1)}, bf16[4,768]{1,0:T(4,128)(2,1)}, u32[]{:S(2)}) copy-start(bf16[4,768]{1,0:T(4,128)(2,1)} %param.13) | copy-start | bytes 18436
  126.3 33.9 %copy-start.2 = (f32[6,128,32]{1,2,0:T(8,128)S(1)}, f32[6,128,32]{1,2,0:T(8,128)}, u32[]{:S(2)}) copy-start(f32[6,128,32]{1,2,0:T(8,128)} %get-tuple-element.35) | copy-start | bytes 294916
  161.0 2.7 %copy-start.6 = (bf16[1536]{0:T(1024)(128)(2,1)S(1)}, bf16[1536]{0:T(1024)(128)(2,1)}, u32[]{:S(2)}) copy-start(bf16[1536]{0:T(1024)(128)(2,1)} %param.17) | copy-start | bytes 9220
  161.0 22.1 %copy-start.1 = (bf16[128,1536]{1,0:T(8,128)(2,1)S(1)}, bf16[128,1536]{1,0:T(8,128)(2,1)}, u32[]{:S(2)}) copy-start(bf16[128,1536]{1,0:T(8,128)(2,1)} %param.16) | copy-start | bytes 1179652
Sparse Core Ops, SparseCore 0:
  163.8 19.2 all-reduce.1
where the time goes:
time: 192 us
  blocking collectives  125 us (65%)
  waiting for transfers between devices  19.4 us (10%)
  between operations  13.6 us (7%)
  other arithmetic  13.3 us (7%)
  local copies, waits for them, and re-layouts  12.9 us (7%)
  matrix products  7.08 us (4%)
    all_gather x1, blocking collectives, local(): lax.all_gather(short_keys, 'seq', axis=0, tiled=True)  32.8 us
    all_gather x1, blocking collectives, local(): lax.all_gather(text_keys, 'seq', axis=0, tiled=True)  31 us
    all_gather x1, blocking collectives, local(): lax.all_gather(short_values, 'seq', axis=0, tiled=True)  31 us
    all_gather x1, blocking collectives, local(): lax.all_gather(text_values, 'seq', axis=0, tiled=True)  30.8 us
    psum x1, waiting for transfers between devices, local(): lax.psum(jnp.dot(attended, out_weight, preferred_element_type=jnp.float32...  19.4 us
  transfers between devices with their start and end apart: 1, of which 1 were waited for; matrix products, arithmetic and copies ran while one was open for 0% of the time, Pallas kernels for 0%

commit v1 on v0

--- a/solution.py
+++ b/solution.py
@@ -6,6 +6,18 @@
 
 HEAD_DIM = 128
 key_block = 512
+
+
+def doubled_up(x, axis, dim):
+    ways, here = (lax.axis_size(axis), lax.axis_index(axis))
+    grown, reach = (x, 1)
+    while reach < ways:
+        theirs = lax.ppermute(grown, axis, [(d, d ^ reach) for d in range(ways)])
+        mine_first = jnp.concatenate([grown, theirs], axis=dim)
+        theirs_first = jnp.concatenate([theirs, grown], axis=dim)
+        grown = jnp.where(here & reach == 0, mine_first, theirs_first)
+        reach = 2 * reach
+    return grown
 
 
 def rope_angles(row_pos, col_pos, head_dim):
@@ -110,7 +122,7 @@
     )
     all_text_keys, all_text_values = (
         lax.all_gather(text_keys, "seq", axis=0, tiled=True),
-        lax.all_gather(text_values, "seq", axis=0, tiled=True),
+        doubled_up(text_values, "seq", 0),
     )
     after_text = absorb(initial, all_text_keys, all_text_values, queries_rot)
     row_max, row_total, accumulated = absorb(

time: 192 us -> 171 us (0.89)
  blocking collectives: 125 us -> 93.7 us
  waiting for transfers between devices: 19.4 us -> 25.9 us
  starting transfers between devices: 0.01 us -> 3.04 us
    all_gather x1 -> x0, blocking collectives: 30.8 us -> none  [local(): lax.all_gather(text_values, 'seq', axis=0, tiled=True)]
    ppermute x0 -> x3, waiting for transfers between devices: none -> 7.64 us  [doubled_up(): theirs = lax.ppermute(grown, axis, [(d, d ^ reach) for d in range(ways)])]
    ppermute x0 -> x3, starting transfers between devices: none -> 3.04 us  [doubled_up(): theirs = lax.ppermute(grown, axis, [(d, d ^ reach) for d in range(ways)])]
  transfers between devices with their start and end apart: 1 -> 4, of which waited for: 1 -> 3; matrix products, arithmetic and copies ran while one was open for 0% -> 17% of each run, Pallas kernels for 0% -> 0%
where the time goes in v1:
time: 171 us
  blocking collectives  93.7 us (55%)
  waiting for transfers between devices  25.9 us (15%)
  local copies, waits for them, and re-layouts  13.7 us (8%)
  between operations  13.7 us (8%)
  other arithmetic  13.5 us (8%)
  matrix products  7.11 us (4%)
  starting transfers between devices  3.04 us (2%)
    all_gather x1, blocking collectives, local(): lax.all_gather(short_keys, 'seq', axis=0, tiled=True)  31.7 us
    all_gather x1, blocking collectives, local(): lax.all_gather(text_keys, 'seq', axis=0, tiled=True)  31 us
    all_gather x1, blocking collectives, local(): lax.all_gather(short_values, 'seq', axis=0, tiled=True)  31 us
    psum x1, waiting for transfers between devices, local(): lax.psum(jnp.dot(attended, out_weight, preferred_element_type=jnp.float32...  18.2 us
    ppermute x3, waiting for transfers between devices, doubled_up(): theirs = lax.ppermute(grown, axis, [(d, d ^ reach) for d in range(ways)])  7.64 us
    dot_general x2, matrix products, absorb_block(): jnp.einsum('hqk,khd->qhd', weights, value_heads, preferred_element_type=j...  3.47 us
    unnamed x27, local copies, waits for them, and re-layouts  3.44 us
  transfers between devices with their start and end apart: 4, of which 3 were waited for; matrix products, arithmetic and copies ran while one was open for 17% of the time, Pallas kernels for 0%

profile of v1, /device:TPU:0, one launch (start us, length us, event | category | flops | bytes accessed | tf_op | source)
XLA Modules:
  0.0 170.7 jit_solution(8012715877196966587)
XLA Ops:
  6.5 3.0 %collective-permute-start = (bf16[4,768]{1,0:T(4,128)(2,1)}, bf16[4,768]{1,0:T(4,128)(2,1)}, u32[]{:S(2)}, u32[]{:S(2)}) collective-permute-start(bf16[4,768]{1,0:T(4,128)(2,1)} %param.13), channel_id=1, source_target_pairs={{0,2},{2,0},{4,6},{6,4},{8,10},{10,8},{12,14},{14,12},{1,3},{3,1},... | collective-permute-start | bytes 18440 | tf_op jit(solution)/shard_map/ppermute | solution.py:15
  10.6 0.7 reshape.270
  11.3 0.8 mul.304
  12.2 0.9 mul.307
  13.0 0.8 mul.310
  13.9 0.8 mul.313
  14.7 1.1 reshape.268
  15.8 1.0 fusion.27
  17.1 1.1 copy.90
  18.2 1.8 %copy.91 = f32[1,32,1,768]{1,3,2,0:T(8,128)} copy(f32[1,32,1,768]{3,2,1,0:T(1,128)} %get-tuple-element.16) | data formatting | bytes 196608
  20.6 0.7 broadcast_multiply_fusion.1
  21.6 3.4 %multiply_add_fusion = f32[32,6,64,2]{0,3,2,1:T(2,128)S(1)} fusion(f32[32,6,64,2]{0,3,2,1:T(2,128)S(1)} %bitcast.86, f32[32,6,64,2]{0,3,2,1:T(2,128)} %bitcast.89, f32[32,6,64,2]{0,3,2,1:T(2,128)S(1)} %bitcast.88, f32[32,6,64,2]{0,3,2,1:T(2,128)S(1)} %bitcast.87, f32[6,64,2]{2,1,0:T(8,128)} %mul.313, f32[6,64,2]{2,1,0:T(8,128)} %mul.310, ...), kind=kLoop, calls=%fused_computation.13 | loop fusion | flops 172032 | bytes 503808 | tf_op jit(solution)/shard_map/add | solution.py:52
  26.2 31.7 %all_gather.10 = bf16[256,768]{1,0:T(8,128)(2,1)S(1)} all-gather(bf16[32,768]{1,0:T(8,128)(2,1)S(1)} %copy.77), channel_id=1, replica_groups=mesh['groups'=2,'seq'=8,'tensor'=2] {'seq'}, dimensions={0}, use_global_device_ids=true | all-gather | bytes 442368 | tf_op jit(solution)/shard_map/all_gather | solution.py:130
  58.4 31.0 %all-gather = bf16[8,4,768]{2,1,0:T(4,128)(2,1)S(1)} all-gather(bf16[1,4,768]{2,1,0:T(4,128)(2,1)} %bitcast.94), channel_id=1, replica_groups=mesh['groups'=2,'seq'=8,'tensor'=2] {'seq'}, dimensions={0}, use_global_device_ids=true | all-gather | bytes 55296 | tf_op jit(solution)/shard_map/all_gather | solution.py:124
  89.4 0.7 reshape.256
  90.0 0.8 broadcast_multiply_fusion.3
  90.8 0.8 fusion.17
  92.6 1.0 fusion.30
  93.6 1.4 fusion.29
  95.0 1.1 reshape.272
  96.5 31.0 %all_gather.11 = bf16[256,768]{1,0:T(8,128)(2,1)S(1)} all-gather(bf16[32,768]{1,0:T(8,128)(2,1)S(1)} %fusion.8), channel_id=1, replica_groups=mesh['groups'=2,'seq'=8,'tensor'=2] {'seq'}, dimensions={0}, use_global_device_ids=true | all-gather | bytes 442368 | tf_op jit(solution)/shard_map/all_gather | solution.py:131
  127.4 0.9 copy.84
  128.4 0.7 broadcast_maximum_fusion
  129.4 2.1 %convolution_bitcast_fusion.1 = f32[128,6,128]{0,2,1:T(8,128)} fusion(bf16[256,6,128]{0,2,1:T(8,128)(2,1)} %bitcast.85, f32[6,128,256]{2,1,0:T(8,128)S(1)} %get-tuple-element.37, f32[6,128]{1,0:T(8,128)S(1)} %get-tuple-element.29), kind=kOutput, calls=%fused_computation.4 | convolution fusion | flops 50724864 | bytes 1575936 | tf_op jit(solution)/shard_map/hqk,khd->qhd/dot_general | solution.py:71
  131.6 0.8 maximum_select_fusion.4
  132.5 0.7 concatenate.64
  133.2 3.0 %collective-permute-done.1 = bf16[8,768]{1,0:T(8,128)(2,1)S(1)} collective-permute-done((bf16[8,768]{1,0:T(8,128)(2,1)S(1)}, bf16[8,768]{1,0:T(8,128)(2,1)S(1)}, u32[]{:S(2)}, u32[]{:S(2)}) %collective-permute-start.1) | collective-permute-done | bytes 12320 | tf_op jit(solution)/shard_map/ppermute | solution.py:15
  136.2 4.7 %collective-permute-done.2 = bf16[16,768]{1,0:T(8,128)(2,1)S(1)} collective-permute-done((bf16[16,768]{1,0:T(8,128)(2,1)S(1)}, bf16[16,768]{1,0:T(8,128)(2,1)S(1)}, u32[]{:S(2)}, u32[]{:S(2)}) %collective-permute-start.2) | collective-permute-done | bytes 24608 | tf_op jit(solution)/shard_map/ppermute | solution.py:15
  141.0 1.4 fusion.4
  142.4 1.2 convolution_convert_fusion
  143.7 18.2 %all-reduce.2.cloned.1.call-done = bf16[128,1536]{1,0:T(8,128)(2,1)} async-done(((bf16[128,1536]{1,0:T(8,128)(2,1)}), bf16[128,1536]{1,0:T(8,128)(2,1)}) %all-reduce.2.cloned.1.call-update) | async-done | bytes 393232 | tf_op jit(solution)/shard_map/psum | solution.py:137
  162.0 1.9 %add_convert_fusion = bf16[128,1536]{1,0:T(8,128)(2,1)} fusion(bf16[128,1536]{1,0:T(8,128)(2,1)} %all-reduce.2.cloned.1.call-done, bf16[128,1536]{1,0:T(8,128)(2,1)S(1)} %copy-done.1, f32[1536]{0:T(1024)S(1)} %convert_element_type.77), kind=kLoop, calls=%fused_computation.10 | loop fusion | flops 983040 | bytes 1185792 | tf_op jit(solution)/shard_map/convert_element_type | solution.py:143
  (58 shorter events, 5.8 us)
Async XLA Ops:
  6.5 135.9 %copy-start = (bf16[768,1536]{1,0:T(8,128)(2,1)S(1)}, bf16[768,1536]{1,0:T(8,128)(2,1)}, u32[]{:S(2)}) copy-start(bf16[768,1536]{1,0:T(8,128)(2,1)} %param.15) | copy-start | bytes 7077892
  6.5 155.4 %all-reduce.2.cloned.1.call-start = ((), (), s32[]{:S(2)}) async-start(), calls=%async_computation | async-start | bytes 786432 | tf_op jit(solution)/shard_map/psum | solution.py:137
  6.5 125.1 %collective-permute-start = (bf16[4,768]{1,0:T(4,128)(2,1)}, bf16[4,768]{1,0:T(4,128)(2,1)}, u32[]{:S(2)}, u32[]{:S(2)}) collective-permute-start(bf16[4,768]{1,0:T(4,128)(2,1)} %param.13), channel_id=1, source_target_pairs={{0,2},{2,0},{4,6},{6,4},{8,10},{10,8},{12,14},{14,12},{1,3},{3,1},... | collective-permute-start | bytes 18440 | tf_op jit(solution)/shard_map/ppermute | solution.py:15
  20.6 1.0 copy-start.10
  25.0 33.1 %copy-start.4 = (bf16[128,768]{1,0:T(8,128)(2,1)S(1)}, bf16[128,768]{1,0:T(8,128)(2,1)}, u32[]{:S(2)}) copy-start(bf16[128,768]{1,0:T(8,128)(2,1)} %param.9) | copy-start | bytes 589828
  90.0 3.5 %copy-start.3 = (bf16[32,6,128]{2,1,0:T(8,128)(2,1)S(1)}, bf16[32,6,128]{2,1,0:T(8,128)(2,1)}, u32[]{:S(2)}) copy-start(bf16[32,6,128]{2,1,0:T(8,128)(2,1)} %reshape.256) | copy-start | bytes 147460
  96.4 35.1 %copy-start.5 = (f32[6,128]{1,0:T(8,128)S(1)}, f32[6,128]{1,0:T(8,128)}, u32[]{:S(2)}) copy-start(f32[6,128]{1,0:T(8,128)} %get-tuple-element.36) | copy-start | bytes 9220
  96.4 35.1 %copy-start.6 = (f32[6,128]{1,0:T(8,128)S(1)}, f32[6,128]{1,0:T(8,128)}, u32[]{:S(2)}) copy-start(f32[6,128]{1,0:T(8,128)} %get-tuple-element.34) | copy-start | bytes 9220
  96.5 35.1 %copy-start.7 = (bf16[4,768]{1,0:T(4,128)(2,1)S(1)}, bf16[4,768]{1,0:T(4,128)(2,1)}, u32[]{:S(2)}) copy-start(bf16[4,768]{1,0:T(4,128)(2,1)} %param.13) | copy-start | bytes 18436
  128.4 3.1 %copy-start.2 = (f32[6,128,32]{1,2,0:T(8,128)S(1)}, f32[6,128,32]{1,2,0:T(8,128)}, u32[]{:S(2)}) copy-start(f32[6,128,32]{1,2,0:T(8,128)} %get-tuple-element.35) | copy-start | bytes 294916
  129.1 2.5 %copy-start.8 = (f32[6,128]{1,0:T(8,128)}, f32[6,128]{1,0:T(8,128)S(1)}, u32[]{:S(2)}) copy-start(f32[6,128]{1,0:T(8,128)S(1)} %get-tuple-element.28) | copy-start | bytes 9220
  132.4 3.8 %collective-permute-start.1 = (bf16[8,768]{1,0:T(8,128)(2,1)S(1)}, bf16[8,768]{1,0:T(8,128)(2,1)S(1)}, u32[]{:S(2)}, u32[]{:S(2)}) collective-permute-start(bf16[8,768]{1,0:T(8,128)(2,1)S(1)} %maximum_select_fusion.4), channel_id=1, source_target_pairs={{0,4},{2,6},{4,0},{6,2},{8,12},{10,14},{12,8},{14,10},{1,5},{3,7},... | collective-permute-start | bytes 36872 | tf_op jit(solution)/shard_map/ppermute | solution.py:15
  136.2 4.7 %collective-permute-start.2 = (bf16[16,768]{1,0:T(8,128)(2,1)S(1)}, bf16[16,768]{1,0:T(8,128)(2,1)S(1)}, u32[]{:S(2)}, u32[]{:S(2)}) collective-permute-start(bf16[16,768]{1,0:T(8,128)(2,1)S(1)} %maximum_select_fusion.2), channel_id=1, source_target_pairs={{0,8},{2,10},{4,12},{6,14},{8,0},{10,2},{12,4},{14,6},{1,9},{3,11}... | collective-permute-start | bytes 73736 | tf_op jit(solution)/shard_map/ppermute | solution.py:15
  141.0 2.7 %copy-start.9 = (bf16[1536]{0:T(1024)(128)(2,1)S(1)}, bf16[1536]{0:T(1024)(128)(2,1)}, u32[]{:S(2)}) copy-start(bf16[1536]{0:T(1024)(128)(2,1)} %param.17) | copy-start | bytes 9220
  141.0 20.9 %copy-start.1 = (bf16[128,1536]{1,0:T(8,128)(2,1)S(1)}, bf16[128,1536]{1,0:T(8,128)(2,1)}, u32[]{:S(2)}) copy-start(bf16[128,1536]{1,0:T(8,128)(2,1)} %param.16) | copy-start | bytes 1179652
Sparse Core Ops, SparseCore 0:
  143.8 18.0 all-reduce.1
